TPU v7x, 128 devices: a whole 4x4x4 slice. The times are simulated.
128 devices in a mesh: tok: 32 (over z, x, y_hi), ch: 4 (over y_lo, core).
Axes of the slice: x: 4, y: 4 (y_hi: 2, y_lo: 2; y = y_hi * 2 + y_lo), z: 4, core: 2. Of those that a mesh axis runs over, the one named last changes fastest.
Arguments:
- tokens: bfloat16 [262144, 1024], P('tok', 'ch'), may hold values from -6 to 6
- w_value: bfloat16 [1024, 1024], P(None, 'ch'), may hold values from -0.1875 to 0.1875
- w_gate: bfloat16 [1024, 1024], P(None, 'ch'), may hold values from -0.1875 to 0.1875
- first_factor: bfloat16 [512, 512], replicated, may hold values from -0.25 to 0.25
- twiddle: float32 [512, 512], P('tok'), may hold values from 0.5 to 1.5
- second_factor: float32 [512, 512], replicated, may hold values from -0.25 to 0.25
- freq_kernel: float32 [512, 1024], P('tok', 'ch'), may hold values from -5 to 5
- row_kernel: float32 [512, 1024], P(None, 'ch'), may hold values from -5 to 5
- inverse_first: float32 [512, 512], replicated, may hold values from -0.25 to 0.25
- inverse_second: float32 [512, 512], replicated, may hold values from -0.25 to 0.25
Outputs:
- mixed: bfloat16 [262144, 1024], P('tok', 'ch')
All inputs are finite; a program needn't handle non-finite values.
Results may differ from a plain program's by a relative error of at most 0.0049.
Values may be sent and summed in bfloat16 or wider, within the bound.
A program may use at most 128 MiB of HBM per device.

v0:
```python
import jax
import jax.numpy as jnp
from jax import lax
from jax.sharding import PartitionSpec as P

BLOCK_B = 512


def shards(
    tokens,
    w_value,
    w_gate,
    first_factor,
    twiddle,
    second_factor,
    freq_kernel,
    row_kernel,
    inverse_first,
    inverse_second,
):
    tok_rows, channels = tokens.shape
    highest = lax.Precision.HIGHEST
    piece = lax.all_gather(tokens, "ch", axis=1, tiled=True)
    value = jnp.dot(piece, w_value, preferred_element_type=jnp.float32)
    gate = jnp.dot(piece, w_gate, preferred_element_type=jnp.float32)
    mixed_in = (value * jax.nn.silu(gate)).astype(jnp.bfloat16)
    local_rows = tok_rows // BLOCK_B
    grid = mixed_in.reshape(local_rows, BLOCK_B, channels)
    section = jnp.einsum("kb,abc->akc", first_factor, grid, preferred_element_type=jnp.float32)
    section = section * twiddle[:, :, None]
    spectrum = jnp.einsum(
        "ja,akc->jkc",
        second_factor,
        lax.all_to_all(section, "tok", split_axis=1, concat_axis=0, tiled=True),
        precision=highest,
    )
    spectrum = spectrum * freq_kernel[None, :, :] * row_kernel[:, None, :]
    spectrum = jnp.einsum("ij,jkc->ikc", inverse_first, spectrum, precision=highest)
    result = jnp.einsum(
        "bk,akc->abc",
        inverse_second,
        lax.all_to_all(spectrum, "tok", split_axis=0, concat_axis=1, tiled=True),
        precision=highest,
    )
    return result.reshape(tok_rows, channels).astype(jnp.bfloat16)


def solution(mesh):
    return jax.shard_map(
        shards,
        mesh=mesh,
        in_specs=(
            P("tok", "ch"),
            P(None, "ch"),
            P(None, "ch"),
            P(),
            P("tok", None),
            P(),
            P("tok", "ch"),
            P(None, "ch"),
            P(),
            P(),
        ),
        out_specs=P("tok", "ch"),
        check_vma=False,
    )
```

profile of v0, /device:TPU:0, one launch (start us, length us, event | category | flops | bytes accessed | tf_op | source)
XLA Modules:
  0.0 576.0 jit_solution(5134124481369577503)
XLA Ops:
  6.5 0.0 copy-start
  6.5 0.0 all-gather.2.cloned.1.call-start
  6.5 0.7 all-gather.2.cloned.1.call-update
  7.3 0.0 copy-start.7
  7.3 153.4 %all-gather.2.cloned.1.call-done = bf16[8192,1024]{1,0:T(8,128)(2,1)} async-done(((bf16[8192,256]{1,0:T(8,128)(2,1)}), bf16[8192,1024]{1,0:T(8,128)(2,1)}) %all-gather.2.cloned.1.call-update) | async-done | bytes 16777232 | tf_op jit(solution)/shard_map/all_gather | solution.py:23
  160.7 13.6 %fusion.12 = f32[8192,256]{1,0:T(8,128)} fusion(bf16[8192,1024]{1,0:T(8,128)(2,1)} %all-gather.2.cloned.1.call-done, bf16[1024,256]{1,0:T(8,128)(2,1)} %param.12), kind=kOutput, calls=%fused_computation.16 | convolution fusion | flops 4294967296 | bytes 25690112 | tf_op jit(solution)/shard_map/dot_general | solution.py:25
  174.2 0.0 copy-done.7
  174.2 0.0 copy-start.3
  174.2 0.0 copy-start.5
  174.2 13.5 %fusion = bf16[8192,256]{1,0:T(8,128)(2,1)S(1)} fusion(bf16[8192,1024]{1,0:T(8,128)(2,1)} %all-gather.2.cloned.1.call-done, bf16[1024,256]{1,0:T(8,128)(2,1)S(1)} %copy-done.7, f32[8192,256]{1,0:T(8,128)} %fusion.12), kind=kOutput, calls=%fused_computation.1 | convolution fusion | flops 4307550208 | bytes 29884416 | tf_op jit(solution)/shard_map/dot_general | solution.py:24
  187.7 0.0 copy-done.3
  187.7 0.0 copy-done.5
  187.7 6.1 %multiply_bitcast_fusion = f32[16,512,256]{1,2,0:T(8,128)} fusion(f32[16,512]{1,0:T(8,128)S(1)} %copy-done.5, bf16[16,512,256]{2,1,0:T(8,128)(2,1)S(1)} %bitcast.42, bf16[512,512]{1,0:T(8,128)(2,1)S(1)} %copy-done.3), kind=kOutput, calls=%fused_computation.7 | convolution fusion | flops 2149580800 | bytes 13139968 | tf_op jit(solution)/shard_map/kb,abc->akc/dot_general | solution.py:29
  193.9 10.3 %copy.23 = f32[16,512,256]{2,0,1:T(8,128)} copy(f32[16,512,256]{1,2,0:T(8,128)} %multiply_bitcast_fusion) | data formatting | bytes 16777216 | tf_op jit(solution)/shard_map/mul | solution.py:30
  204.2 0.0 copy-start.4
  204.2 10.2 %all-to-all-start = ((f32[16,512,256]{2,0,1:T(8,128)}), f32[16,512,256]{2,0,1:T(8,128)}, u32[]{:S(2)}, u32[]{:S(2)}) async-start(f32[16,512,256]{2,0,1:T(8,128)} %copy.23), calls=%async_computation | async-start | bytes 16777216 | tf_op jit(solution)/shard_map/all_to_all | solution.py:34
  214.4 0.0 copy-done.4
  214.4 0.2 copy.27
  214.6 130.6 %all-to-all-done = f32[16,512,256]{2,0,1:T(8,128)} async-done(((f32[16,512,256]{2,0,1:T(8,128)}), f32[16,512,256]{2,0,1:T(8,128)}, u32[]{:S(2)}, u32[]{:S(2)}) %all-to-all-start) | async-done | bytes 8388640 | tf_op jit(solution)/shard_map/all_to_all | solution.py:34
  345.1 10.9 %copy.25 = f32[32,16,16,256]{3,2,1,0:T(8,128)S(1)} copy(f32[32,16,16,256]{3,1,2,0:T(8,128)} %bitcast.5) | data formatting | bytes 16777216 | tf_op jit(solution)/shard_map/all_to_all | solution.py:34
  356.1 0.0 copy-done
  356.1 0.0 copy-start.1
  356.1 0.0 copy-start.6
  356.1 30.9 %fusion.2 = f32[16,256,512]{2,1,0:T(8,128)S(1)} fusion(f32[512,16,256]{2,1,0:T(8,128)S(1)} %bitcast.40, f32[512,512]{1,0:T(8,128)S(1)} %copy-done), kind=kOutput, calls=%fused_computation.4 | convolution fusion | flops 12884901888 | bytes 17825792 | tf_op jit(solution)/shard_map/ja,akc->jkc/dot_general | solution.py:31
  387.0 0.0 copy-done.1
  387.0 0.0 copy-done.6
  387.0 16.4 %fusion.7 = f32[512,16,256]{0,2,1:T(8,128)} fusion(f32[16,256,512]{2,1,0:T(8,128)S(1)} %fusion.2, f32[512,256]{0,1:T(8,128)S(1)} %copy.27, f32[16,256]{1,0:T(8,128)S(1)} %copy-done.6, f32[512,512]{1,0:T(8,128)S(1)} %copy-done.1), kind=kOutput, calls=%fused_computation.11 | convolution fusion | flops 12889096192 | bytes 18366464 | tf_op jit(solution)/shard_map/ij,jkc->ikc/dot_general | solution.py:38
  403.5 10.3 %copy.28 = f32[512,16,256]{2,1,0:T(8,128)} copy(f32[512,16,256]{0,2,1:T(8,128)} %fusion.7) | data formatting | bytes 16777216 | tf_op jit(solution)/shard_map/ij,jkc->ikc/dot_general | solution.py:38
  413.7 118.4 %all_to_all.36 = f32[512,16,256]{2,1,0:T(8,128)S(1)} all-to-all(f32[512,16,256]{2,1,0:T(8,128)} %copy.28), channel_id=1, replica_groups=mesh['tok'=32,'ch'=4] {'tok'}, dimensions={0} | all-to-all | bytes 16777216 | tf_op jit(solution)/shard_map/all_to_all | solution.py:42
  532.2 0.0 copy-start.2
  532.2 1.4 copy.29
  533.6 0.0 copy-done.2
  533.6 29.0 %convert_bitcast_fusion = bf16[16,512,256]{1,2,0:T(8,128)(2,1)} fusion(f32[16,512,256]{2,1,0:T(8,128)S(1)} %bitcast.39, f32[512,512]{1,0:T(8,128)S(1)} %copy-done.2), kind=kOutput, calls=%fused_computation.8 | convolution fusion | flops 12886999040 | bytes 13631488 | tf_op jit(solution)/shard_map/bk,akc->abc/dot_general | solution.py:39
  562.6 6.4 %copy.31 = bf16[16,512,256]{2,1,0:T(8,128)(2,1)} copy(bf16[16,512,256]{1,2,0:T(8,128)(2,1)} %convert_bitcast_fusion) | data formatting | bytes 8388608 | tf_op jit(solution)/shard_map/convert_element_type | solution.py:45
Async XLA Ops:
  6.5 349.6 %copy-start = (f32[512,512]{1,0:T(8,128)S(1)}, f32[512,512]{1,0:T(8,128)}, u32[]{:S(2)}) copy-start(f32[512,512]{1,0:T(8,128)} %param.15) | copy-start | bytes 3145732
  6.5 154.1 %all-gather.2.cloned.1.call-start = ((), (), s32[]{:S(2)}) async-start(), calls=%async_computation.2 | async-start | bytes 20971520 | tf_op jit(solution)/shard_map/all_gather | solution.py:23
  7.3 167.0 %copy-start.7 = (bf16[1024,256]{1,0:T(8,128)(2,1)S(1)}, bf16[1024,256]{1,0:T(8,128)(2,1)}, u32[]{:S(2)}) copy-start(bf16[1024,256]{1,0:T(8,128)(2,1)} %param.11) | copy-start | bytes 1572868
  174.2 13.5 %copy-start.3 = (bf16[512,512]{1,0:T(8,128)(2,1)S(1)}, bf16[512,512]{1,0:T(8,128)(2,1)}, u32[]{:S(2)}) copy-start(bf16[512,512]{1,0:T(8,128)(2,1)} %param.13) | copy-start | bytes 1572868
  174.2 13.5 %copy-start.5 = (f32[16,512]{1,0:T(8,128)S(1)}, f32[16,512]{1,0:T(8,128)}, u32[]{:S(2)}) copy-start(f32[16,512]{1,0:T(8,128)} %param.14) | copy-start | bytes 98308
  204.2 10.2 %copy-start.4 = (f32[512,256]{1,0:T(8,128)S(1)}, f32[512,256]{1,0:T(8,128)}, u32[]{:S(2)}) copy-start(f32[512,256]{1,0:T(8,128)} %param.17) | copy-start | bytes 1572868
  204.2 141.0 %all-to-all-start = ((f32[16,512,256]{2,0,1:T(8,128)}), f32[16,512,256]{2,0,1:T(8,128)}, u32[]{:S(2)}, u32[]{:S(2)}) async-start(f32[16,512,256]{2,0,1:T(8,128)} %copy.23), calls=%async_computation | async-start | bytes 16777216 | tf_op jit(solution)/shard_map/all_to_all | solution.py:34
  356.1 30.9 %copy-start.1 = (f32[512,512]{1,0:T(8,128)S(1)}, f32[512,512]{1,0:T(8,128)}, u32[]{:S(2)}) copy-start(f32[512,512]{1,0:T(8,128)} %param.18) | copy-start | bytes 3145732
  356.1 30.9 %copy-start.6 = (f32[16,256]{1,0:T(8,128)S(1)}, f32[16,256]{1,0:T(8,128)}, u32[]{:S(2)}) copy-start(f32[16,256]{1,0:T(8,128)} %param.16) | copy-start | bytes 49156
  532.2 1.4 copy-start.2
Sparse Core Ops, SparseCore 0:
  9.0 151.6 all-gather.1
where the time goes:
time: 588 us; the launch traced here: 576 us
  waiting for transfers between devices  285 us (48%)
  blocking collectives  118 us (20%)
  matrix products  109 us (19%)
  local copies, waits for them, and re-layouts  39.6 us (7%)
  between operations  13.7 us (2%)
  starting transfers between devices  10.2 us (2%)
    all_gather x1, waiting for transfers between devices, shards(): piece = lax.all_gather(tokens, 'ch', axis=1, tiled=True)  153 us
    all_to_all x1, waiting for transfers between devices, shards(): lax.all_to_all(section, 'tok', split_axis=1, concat_axis=0, tiled=True)  131 us
    all_to_all x1, blocking collectives, shards(): lax.all_to_all(spectrum, 'tok', split_axis=0, concat_axis=1, tiled=True)  118 us
    dot_general x1, matrix products, shards(): jnp.einsum('ja,akc->jkc', second_factor, lax.all_to_all(section, 'tok', s...  30.9 us
    dot_general x1, matrix products, shards(): jnp.einsum('bk,akc->abc', inverse_second, lax.all_to_all(spectrum, 'tok',...  29 us
    dot_general x1, matrix products, shards(): jnp.einsum('ij,jkc->ikc', inverse_first, spectrum, precision=highest)  16.4 us
    dot_general x1, matrix products, shards(): gate = jnp.dot(piece, w_gate, preferred_element_type=jnp.float32)  13.6 us
    dot_general x1, matrix products, shards(): value = jnp.dot(piece, w_value, preferred_element_type=jnp.float32)  13.5 us
  transfers between devices with their start and end apart: 2, of which 2 were waited for; matrix products, arithmetic and copies ran while one was open for 0% of the time, Pallas kernels for 0%

commit v1 on v0

v1 whole, which is shorter than its diff:
```python
import jax
import jax.numpy as jnp
from jax import lax
from jax.sharding import PartitionSpec as P

BLOCK_B = 512


def shards(
    tokens,
    w_value,
    w_gate,
    first_factor,
    twiddle,
    second_factor,
    freq_kernel,
    row_kernel,
    inverse_first,
    inverse_second,
):
    tok_rows, channels = tokens.shape
    n_tok, n_ch = lax.axis_size("tok"), lax.axis_size("ch")
    f32, bf16 = jnp.float32, jnp.bfloat16
    wide = channels * n_ch
    my_ch = lax.axis_index("ch")
    piece = lax.all_to_all(tokens, "ch", split_axis=0, concat_axis=1, tiled=True)
    weights = lax.all_gather(jnp.concatenate([w_value, w_gate], axis=1), "ch", axis=0)
    both = jnp.einsum("nd,hdc->nhc", piece, weights, preferred_element_type=f32)
    value, gate = both[:, :, :channels], both[:, :, channels:]
    rows = tok_rows // BLOCK_B // n_ch
    gated = (value * jax.nn.silu(gate)).astype(bf16).reshape(rows, BLOCK_B, wide)
    my_twiddle = lax.dynamic_slice_in_dim(twiddle, my_ch * rows, rows, 0)
    section = jnp.einsum("kb,abc->akc", first_factor, gated, preferred_element_type=f32)
    section = (section * my_twiddle[:, :, None]).astype(bf16)
    k_rows = BLOCK_B // n_tok
    section = section.reshape(rows, n_tok, k_rows, n_ch, channels).transpose(1, 3, 0, 2, 4)
    section = section.reshape(n_tok * n_ch, rows, k_rows, channels)
    section = lax.all_to_all(section, ("tok", "ch"), split_axis=0, concat_axis=0, tiled=True)
    section = section.reshape(n_tok * n_ch * rows, k_rows, channels)
    spectrum = jnp.einsum("ja,akc->jkc", second_factor.astype(bf16), section, preferred_element_type=f32)
    spectrum = (spectrum * freq_kernel[None, :, :] * row_kernel[:, None, :]).astype(bf16)
    spectrum = jnp.einsum("ij,jkc->ikc", inverse_first.astype(bf16), spectrum, preferred_element_type=f32)
    spectrum = lax.all_to_all(spectrum.astype(bf16), "tok", split_axis=0, concat_axis=1, tiled=True)
    result = jnp.einsum("bk,akc->abc", inverse_second.astype(bf16), spectrum, preferred_element_type=f32)
    return result.reshape(tok_rows, channels).astype(bf16)


def solution(mesh):
    return jax.shard_map(
        shards,
        mesh=mesh,
        in_specs=(
            P("tok", "ch"),
            P(None, "ch"),
            P(None, "ch"),
            P(),
            P("tok", None),
            P(),
            P("tok", "ch"),
            P(None, "ch"),
            P(),
            P(),
        ),
        out_specs=P("tok", "ch"),
        check_vma=False,
    )
```

time: 588 us -> 318 us (0.54); the launches traced: 576 us -> 317 us
  waiting for transfers between devices: 285 us -> 134 us
  matrix products: 109 us -> 31.3 us
  blocking collectives: 118 us -> 57.2 us
  local copies, waits for them, and re-layouts: 39.6 us -> 58.7 us
  starting transfers between devices: 10.2 us -> 16.5 us
  other arithmetic: 0 us -> 6.21 us
    all_gather x1, waiting for transfers between devices: 153 us -> 0.01 us  [shards(): lax.all_gather(jnp.concatenate([w_value, w_gate], axis=1), 'ch', axis=0)]
    dot_general x6 -> x4, matrix products: 109 us -> 31.3 us  [the longest x1 12 us: shards(): both = jnp.einsum('nd,hdc->nhc', piece, weights, preferred_element_type=f32)]
    all_to_all x1, blocking collectives: 118 us -> 57.2 us  [shards(): lax.all_to_all(spectrum.astype(bf16), 'tok', split_axis=0, concat_axis=1,...]
    reshape x0 -> x2, local copies, waits for them, and re-layouts: none -> 15.6 us  [the longest x1 7.83 us: shards(): section.reshape(rows, n_tok, k_rows, n_ch, channels)]
    convert_element_type x1 -> x3, local copies, waits for them, and re-layouts: 6.38 us -> 20.5 us  [the longest x1 7.86 us: shards(): spectrum.astype(bf16)]
    mul x1 -> x0, local copies, waits for them, and re-layouts: 10.3 us -> none  [shards(): section = section * twiddle[:, :, None]]
    dot_general x1 -> x0, local copies, waits for them, and re-layouts: 10.3 us -> none  [shards(): jnp.einsum('ij,jkc->ikc', inverse_first, spectrum, precision=highest)]
    all_to_all x1 -> x2, starting transfers between devices: 10.2 us -> 16.5 us  [the longest x1 11.7 us: shards(): lax.all_to_all(section, ('tok', 'ch'), split_axis=0, concat_axis=0, tiled...]
  transfers between devices with their start and end apart: 2 -> 3, of which waited for: 2 -> 2; matrix products, arithmetic and copies ran while one was open for 0% -> 5% of each run, Pallas kernels for 0% -> 0%
where the time goes in v1:
time: 318 us; the launch traced here: 317 us
  waiting for transfers between devices  134 us (42%)
  local copies, waits for them, and re-layouts  58.7 us (18%)
  blocking collectives  57.2 us (18%)
  matrix products  31.3 us (10%)
  starting transfers between devices  16.5 us (5%)
  between operations  13.5 us (4%)
  other arithmetic  6.21 us (2%)
    all_to_all x1, waiting for transfers between devices, shards(): lax.all_to_all(tokens, 'ch', split_axis=0, concat_axis=1, tiled=True)  81.2 us
    all_to_all x1, blocking collectives, shards(): lax.all_to_all(spectrum.astype(bf16), 'tok', split_axis=0, concat_axis=1,...  57.2 us
    all_to_all x1, waiting for transfers between devices, shards(): lax.all_to_all(section, ('tok', 'ch'), split_axis=0, concat_axis=0, tiled...  52.3 us
    all_to_all x2, local copies, waits for them, and re-layouts, shards(): lax.all_to_all(tokens, 'ch', split_axis=0, concat_axis=1, tiled=True)  15.3 us
    dot_general x1, matrix products, shards(): both = jnp.einsum('nd,hdc->nhc', piece, weights, preferred_element_type=f32)  12 us
    all_to_all x1, starting transfers between devices, shards(): lax.all_to_all(section, ('tok', 'ch'), split_axis=0, concat_axis=0, tiled...  11.7 us
    dot_general x1, matrix products, shards(): jnp.einsum('ij,jkc->ikc', inverse_first.astype(bf16), spectrum, preferred...  8.25 us
    convert_element_type x1, local copies, waits for them, and re-layouts, shards(): spectrum.astype(bf16)  7.86 us
  transfers between devices with their start and end apart: 3, of which 2 were waited for; matrix products, arithmetic and copies ran while one was open for 5% of the time, Pallas kernels for 0%

profile of v1, /device:TPU:0, one launch (start us, length us, event | category | flops | bytes accessed | tf_op | source)
XLA Modules:
  0.0 317.0 jit_solution(1236276943918999403)
XLA Ops:
  6.5 0.0 copy-start
  6.5 0.0 all-gather.3.cloned.1.call-start
  6.5 2.4 pad_maximum_fusion
  8.9 0.0 all-gather.3.cloned.1.call-update
  9.0 4.8 %all-to-all-start = ((bf16[4,2048,256]{2,1,0:T(8,128)(2,1)}), bf16[4,2048,256]{2,1,0:T(8,128)(2,1)}, u32[]{:S(2)}, u32[]{:S(2)}) async-start(bf16[4,2048,256]{2,1,0:T(8,128)(2,1)} %bitcast.47), calls=%async_computation | async-start | bytes 8388608 | tf_op jit(solution)/shard_map/all_to_all | solution.py:26
  13.8 0.7 constant_dynamic-slice_fusion
  14.6 81.2 %all-to-all-done = bf16[4,2048,256]{2,1,0:T(8,128)(2,1)} async-done(((bf16[4,2048,256]{2,1,0:T(8,128)(2,1)}), bf16[4,2048,256]{2,1,0:T(8,128)(2,1)}, u32[]{:S(2)}, u32[]{:S(2)}) %all-to-all-start) | async-done | bytes 4194336 | tf_op jit(solution)/shard_map/all_to_all | solution.py:26
  95.8 7.6 %copy.36 = bf16[2048,4,256]{2,1,0:T(4,128)(2,1)} copy(bf16[2048,4,256]{2,0,1:T(8,128)(2,1)} %bitcast.2) | data formatting | bytes 8388608 | tf_op jit(solution)/shard_map/all_to_all | solution.py:26
  103.3 7.7 %reshape.25 = bf16[2048,1024,1]{1,0,2:T(8,128)(2,1)} reshape(bf16[2048,4,256]{2,1,0:T(4,128)(2,1)} %copy.36) | data formatting | bytes 8388608 | tf_op jit(solution)/shard_map/all_to_all | solution.py:26
  111.1 0.0 all-gather.3.cloned.1.call-done
  111.1 12.0 %convolution_bitcast_fusion = f32[2048,4,512]{0,2,1:T(8,128)S(1)} fusion(bf16[4,1024,512]{2,1,0:T(8,128)(2,1)} %bitcast.49, bf16[2048,1024,1]{1,0,2:T(8,128)(2,1)} %reshape.25), kind=kOutput, calls=%fused_computation.5 | convolution fusion | flops 8589934592 | bytes 25165824 | tf_op jit(solution)/shard_map/nd,hdc->nhc/dot_general | solution.py:28
  123.1 3.8 %fusion = bf16[2048,4,256]{0,2,1:T(8,128)(2,1)} fusion(f32[2048,4,512]{0,2,1:T(8,128)S(1)} %convolution_bitcast_fusion), kind=kLoop, calls=%fused_computation.1 | loop fusion | flops 12582912 | bytes 20971520 | tf_op jit(solution)/shard_map/convert_element_type | solution.py:31
  126.9 7.8 %reshape.20 = bf16[4,512,1024]{1,0,2:T(4,128)(2,1)} reshape(bf16[2048,4,256]{0,2,1:T(8,128)(2,1)} %fusion) | data formatting | bytes 8388608 | tf_op jit(solution)/shard_map/reshape | solution.py:31
  134.7 0.0 copy-done
  134.7 6.6 %fusion.2 = bf16[4,512,1024]{1,2,0:T(8,128)(2,1)} fusion(f32[4,512]{1,0:T(4,128)S(1)} %constant_dynamic-slice_fusion, bf16[4,512,1024]{1,0,2:T(4,128)(2,1)} %reshape.20, bf16[512,512]{1,0:T(8,128)(2,1)S(1)} %copy-done), kind=kOutput, calls=%fused_computation.6 | convolution fusion | flops 2151677952 | bytes 8921088 | tf_op jit(solution)/shard_map/kb,abc->akc/dot_general | solution.py:33
  141.3 6.3 %copy.39 = bf16[4,512,1024]{2,1,0:T(8,128)(2,1)} copy(bf16[4,512,1024]{1,2,0:T(8,128)(2,1)} %fusion.2) | data formatting | bytes 8388608 | tf_op jit(solution)/shard_map/convert_element_type | solution.py:34
  147.6 7.8 %reshape.21 = bf16[4,32,16,4,256]{4,3,2,1,0:T(4,128)(2,1)} reshape(bf16[4,512,1024]{2,1,0:T(8,128)(2,1)} %copy.39) | data formatting | bytes 8388608 | tf_op jit(solution)/shard_map/reshape | solution.py:36
  155.4 5.1 %copy.40 = bf16[32,4,4,16,256]{4,3,2,1,0:T(8,128)(2,1)} copy(bf16[32,4,4,16,256]{4,1,3,0,2:T(4,128)(2,1)} %bitcast.45) | data formatting | bytes 8388608 | tf_op jit(solution)/shard_map/transpose | solution.py:36
  160.5 0.0 copy-start.2
  160.5 0.0 copy-start.3
  160.5 0.0 copy-start.4
  160.5 0.0 copy-start.6
  160.5 11.7 %all-to-all-start.1 = ((bf16[128,4,16,256]{3,2,1,0:T(8,128)(2,1)}), bf16[128,4,16,256]{3,2,1,0:T(8,128)(2,1)}, u32[]{:S(2)}, u32[]{:S(2)}) async-start(bf16[128,4,16,256]{3,2,1,0:T(8,128)(2,1)} %bitcast.44), calls=%async_computation.1 | async-start | bytes 8388608 | tf_op jit(solution)/shard_map/all_to_all | solution.py:38
  172.2 0.0 copy-done.2
  172.2 0.2 copy.42
  172.4 52.3 %all-to-all-done.1 = bf16[128,4,16,256]{3,2,1,0:T(8,128)(2,1)} async-done(((bf16[128,4,16,256]{3,2,1,0:T(8,128)(2,1)}), bf16[128,4,16,256]{3,2,1,0:T(8,128)(2,1)}, u32[]{:S(2)}, u32[]{:S(2)}) %all-to-all-start.1) | async-done | bytes 4194336 | tf_op jit(solution)/shard_map/all_to_all | solution.py:38
  224.7 0.0 copy-done.3
  224.7 0.0 copy-done.4
  224.7 0.0 copy-done.6
  224.7 8.3 %convert_bitcast_fusion.1 = bf16[512,16,256]{0,2,1:T(8,128)(2,1)} fusion(f32[512,256]{0,1:T(8,128)S(1)} %copy.42, f32[16,256]{1,0:T(8,128)S(1)} %copy-done.6, bf16[512,16,256]{2,1,0:T(8,128)(2,1)} %bitcast.8, f32[512,512]{1,0:T(8,128)S(1)} %copy-done.3, f32[512,512]{1,0:T(8,128)S(1)} %copy-done.4), kind=kOutput, calls=%fused_computation.13 | convolution fusion | flops 4303880192 | bytes 11026432 | tf_op jit(solution)/shard_map/ij,jkc->ikc/dot_general | solution.py:42
  233.0 7.9 %copy.43 = bf16[512,16,256]{2,1,0:T(8,128)(2,1)} copy(bf16[512,16,256]{0,2,1:T(8,128)(2,1)} %convert_bitcast_fusion.1) | data formatting | bytes 8388608 | tf_op jit(solution)/shard_map/convert_element_type | solution.py:43
  240.8 57.2 %all_to_all.42 = bf16[512,16,256]{2,1,0:T(8,128)(2,1)S(1)} all-to-all(bf16[512,16,256]{2,1,0:T(8,128)(2,1)} %copy.43), channel_id=1, replica_groups=mesh['tok'=32,'ch'=4] {'tok'}, dimensions={0} | all-to-all | bytes 8388608 | tf_op jit(solution)/shard_map/all_to_all | solution.py:43
  298.1 0.0 copy-start.5
  298.1 0.4 copy.44
  298.5 0.8 copy-done.5
  299.3 0.0 copy-start.1
  299.3 4.4 %convert_bitcast_fusion = bf16[16,512,256]{1,2,0:T(8,128)(2,1)} fusion(bf16[16,512,256]{2,1,0:T(8,128)(2,1)S(1)} %bitcast.48, f32[512,512]{1,0:T(8,128)S(1)} %copy-done.5), kind=kOutput, calls=%fused_computation.12 | convolution fusion | flops 2149842944 | bytes 9437184 | tf_op jit(solution)/shard_map/bk,akc->abc/dot_general | solution.py:44
  303.7 6.4 %copy.46 = bf16[16,512,256]{2,1,0:T(8,128)(2,1)} copy(bf16[16,512,256]{1,2,0:T(8,128)(2,1)} %convert_bitcast_fusion) | data formatting | bytes 8388608 | tf_op jit(solution)/shard_map/convert_element_type | solution.py:45
  310.1 0.0 copy-done.1
Async XLA Ops:
  6.5 128.2 %copy-start = (bf16[512,512]{1,0:T(8,128)(2,1)S(1)}, bf16[512,512]{1,0:T(8,128)(2,1)}, u32[]{:S(2)}) copy-start(bf16[512,512]{1,0:T(8,128)(2,1)} %param.13) | copy-start | bytes 1572868
  6.5 104.5 %all-gather.3.cloned.1.call-start = ((), (), s32[]{:S(2)}) async-start(), calls=%async_computation.3 | async-start | bytes 5242880 | tf_op jit(solution)/shard_map/all_gather | solution.py:27
  9.0 86.8 %all-to-all-start = ((bf16[4,2048,256]{2,1,0:T(8,128)(2,1)}), bf16[4,2048,256]{2,1,0:T(8,128)(2,1)}, u32[]{:S(2)}, u32[]{:S(2)}) async-start(bf16[4,2048,256]{2,1,0:T(8,128)(2,1)} %bitcast.47), calls=%async_computation | async-start | bytes 8388608 | tf_op jit(solution)/shard_map/all_to_all | solution.py:26
  160.5 11.7 %copy-start.2 = (f32[512,256]{1,0:T(8,128)S(1)}, f32[512,256]{1,0:T(8,128)}, u32[]{:S(2)}) copy-start(f32[512,256]{1,0:T(8,128)} %param.17) | copy-start | bytes 1572868
  160.5 64.2 %copy-start.3 = (f32[512,512]{1,0:T(8,128)S(1)}, f32[512,512]{1,0:T(8,128)}, u32[]{:S(2)}) copy-start(f32[512,512]{1,0:T(8,128)} %param.18) | copy-start | bytes 3145732
  160.5 64.2 %copy-start.4 = (f32[512,512]{1,0:T(8,128)S(1)}, f32[512,512]{1,0:T(8,128)}, u32[]{:S(2)}) copy-start(f32[512,512]{1,0:T(8,128)} %param.15) | copy-start | bytes 3145732
  160.5 64.2 %copy-start.6 = (f32[16,256]{1,0:T(8,128)S(1)}, f32[16,256]{1,0:T(8,128)}, u32[]{:S(2)}) copy-start(f32[16,256]{1,0:T(8,128)} %param.16) | copy-start | bytes 49156
  160.5 64.2 %all-to-all-start.1 = ((bf16[128,4,16,256]{3,2,1,0:T(8,128)(2,1)}), bf16[128,4,16,256]{3,2,1,0:T(8,128)(2,1)}, u32[]{:S(2)}, u32[]{:S(2)}) async-start(bf16[128,4,16,256]{3,2,1,0:T(8,128)(2,1)} %bitcast.44), calls=%async_computation.1 | async-start | bytes 8388608 | tf_op jit(solution)/shard_map/all_to_all | solution.py:38
  298.1 1.2 copy-start.5
  299.3 10.8 %copy-start.1 = (bf16[512,512]{1,0:T(8,128)(2,1)S(1)}, bf16[512,512]{1,0:T(8,128)(2,1)}, u32[]{:S(2)}) copy-start(bf16[512,512]{1,0:T(8,128)(2,1)} %param.13) | copy-start | bytes 1572868
Sparse Core Ops, SparseCore 0:
  9.1 83.0 all-gather.2

commit v2 on v0

v2 whole, which is shorter than its diff:
```python
import functools

import jax
import jax.numpy as jnp
from jax import lax
from jax.experimental import pallas as pl
from jax.experimental.pallas import tpu as pltpu
from jax.sharding import PartitionSpec as P

MESH = pl.DeviceIdType.MESH
LANES = 128
F32, BF16 = jnp.float32, jnp.bfloat16


def dot(a, b):
    return jnp.dot(a, b, preferred_element_type=F32)


def mixer(
    n_tok,
    tokens, w_value, w_gate, first, twiddle, second, inv_one, inv_two, freq, row_kernel,
    out,
    x, w, sec_out, sec_in, wide_in, wide_out, spec_out, spec_in, result,
    wide_mats, mats,
    cross_s, cross_r, core_s, core_r, fwd_s, fwd_r, own_sem, w_sem, ws_sem, wr_sem, mat_sem,
    a_send, a_recv, a_own, b_send, b_recv, b_own, out_sem,
):
    t, h = lax.axis_index("tok"), lax.axis_index("ch")
    lo, core = h // 2, h % 2
    half, pieces, block, width = x.shape
    n_k = sec_in.shape[1]
    n_a = sec_in.shape[0]
    local = 2 * half
    y_dev = (t, (1 - lo) * 2 + core)
    core_dev = (t, lo * 2 + 1 - core)
    w_dev = (t + 1 - 2 * (t % 2), (1 - lo) * 2 + core)
    far, far_core, near = (1 - lo) * 2 + core, (1 - lo) * 2 + 1 - core, lo * 2 + 1 - core

    barrier = pltpu.get_barrier_semaphore()
    me = t * 2 + lo

    @pl.loop(1, 2 * n_tok)
    def _(j):
        p = (me + j) % (2 * n_tok)
        pl.semaphore_signal(barrier, inc=1, device_id=(p // 2, (p % 2) * 2 + core), device_id_type=MESH)

    pl.semaphore_signal(barrier, inc=1, device_id=core_dev, device_id_type=MESH)
    pl.semaphore_wait(barrier, 2 * n_tok)

    def remote(src, dst, s, r, dev):
        return pltpu.make_async_remote_copy(
            src_ref=src, dst_ref=dst, send_sem=s, recv_sem=r, device_id=dev, device_id_type=MESH
        )

    def rows(at, r):
        return tokens.at[pl.ds(pl.multiple_of((at * half + r) * block, block), block), :]

    def cross(r):
        return remote(rows(1 - lo, r), x.at[r, h], cross_s.at[r], cross_r.at[r], y_dev)

    def partner(r):
        return remote(rows(lo, r), x.at[r, h], core_s.at[r], core_r.at[r], core_dev)

    def own(r):
        return pltpu.make_async_copy(rows(lo, r), x.at[r, h], own_sem.at[r])

    def forward(r):
        return remote(x.at[r, far], x.at[r, far], fwd_s.at[r], fwd_r.at[r], core_dev)

    def w_own(i):
        return pltpu.make_async_copy((w_value, w_gate)[i], w.at[lo, i], w_sem.at[i])

    def w_far(i):
        return remote((w_value, w_gate)[i], w.at[lo, i], ws_sem.at[i], wr_sem.at[i], w_dev)

    def arrived(r, piece, sem):
        pltpu.make_async_copy(x.at[r, piece], x.at[r, piece], sem.at[r]).wait()

    for i in range(2):
        w_own(i).start()
        w_far(i).start()

    @pl.loop(0, half)
    def _(r):
        cross(r).start()
        own(r).start()
        partner(r).start()

    square = (second, inv_one, inv_two)
    for i in range(3):
        pltpu.make_async_copy(square[i], wide_mats.at[i], mat_sem.at[i]).start()
    for i in range(3):
        pltpu.make_async_copy(square[i], wide_mats.at[i], mat_sem.at[i]).wait()
        mats[i] = wide_mats[i].astype(BF16)
    for i in range(2):
        w_own(i).wait()

    tw_lane = lax.broadcasted_iota(jnp.int32, twiddle.shape, 1)

    def project(step):
        q = half // 2
        early = step < q
        middle = (step >= q) & (step < 2 * q)
        late = step - 2 * q
        r = jnp.where(early, step, jnp.where(middle, step - q, q + late // 2))
        other = jnp.where(early, 0, jnp.where(middle, 1, late % 2))
        l = lo + other - 2 * lo * other

        @pl.when(step == q)
        def _():
            for i in range(2):
                pltpu.make_async_copy(w.at[1 - lo, i], w.at[1 - lo, i], wr_sem.at[i]).wait()

        @pl.when(other == 0)
        def _():
            arrived(r, far, cross_r)
            forward(r).start()
            own(r).wait()
            arrived(r, near, core_r)
            arrived(r, far_core, fwd_r)

        row = jnp.concatenate([x[r, p] for p in range(pieces)], axis=1)
        value = dot(row, w[l, 0])
        gate = dot(row, w[l, 1])
        gated = (value * (gate / (1.0 + jnp.exp(-gate)))).astype(BF16)
        scale = jnp.sum(jnp.where(tw_lane == lo * half + r, twiddle[...], 0.0), axis=1, keepdims=True)
        sec_out[r, l] = (dot(first[...], gated) * scale).astype(BF16)

        @pl.when(other == 1)
        def _():
            to = t * local + lo * half + r

            @pl.loop(1, 2 * n_tok)
            def _(j):
                p = (me + j * 27) % (2 * n_tok)
                pt, pl_ = p // 2, p % 2
                remote(
                    sec_out.at[r, pl_, pl.ds(pl.multiple_of(pt * n_k, n_k), n_k), :],
                    sec_in.at[to], a_send, a_recv, (pt, pl_ * 2 + core),
                ).start()

            pltpu.make_async_copy(
                sec_out.at[r, lo, pl.ds(pl.multiple_of(t * n_k, n_k), n_k), :], sec_in.at[to], a_own
            ).start()

    pl.loop(0, 2 * half)(project)

    pltpu.make_async_copy(sec_in.at[pl.ds(0, half)], sec_in.at[pl.ds(0, half)], a_own).wait()
    most = n_a - half
    pltpu.make_async_copy(sec_in.at[pl.ds(0, most)], sec_in.at[pl.ds(0, most)], a_recv).wait()

    step_a = 32
    n_half = width // LANES

    def spread(q):
        lanes = pl.ds(pl.multiple_of(q * LANES, LANES), LANES)

        @pl.loop(0, n_a // step_a)
        def _(i):
            part = sec_in[pl.ds(i * step_a, step_a), :, lanes].astype(F32)
            wide_in[pl.ds(pl.multiple_of(i * step_a * n_k, step_a * n_k), step_a * n_k), :] = part.reshape(
                step_a * n_k, LANES
            )

        @pl.loop(0, n_k // 2)
        def _(kp):
            two = [wide_in[pl.ds(2 * kp + i, n_a, stride=n_k), :].astype(BF16) for i in range(2)]
            mid = dot(mats[0], jnp.concatenate(two, axis=1))
            scale = [freq[2 * kp + i, q] * row_kernel[:, lanes] for i in range(2)]
            mid = (mid * jnp.concatenate(scale, axis=1)).astype(BF16)
            end = dot(mats[1], mid)
            for i in range(2):
                wide_out[pl.ds(2 * kp + i, n_a, stride=n_k), :] = end[:, i * LANES : (i + 1) * LANES]

        @pl.loop(0, n_tok)
        def _(j):
            pt = (t + j * 13) % n_tok
            rows_out = pl.ds(pl.multiple_of(pt * local, local), local)
            flat = pl.ds(pl.multiple_of(pt * local * n_k, local * n_k), local * n_k)
            spec_out[q, rows_out] = wide_out[flat, :].astype(BF16).reshape(local, n_k, LANES)
            at = pl.ds(pl.multiple_of(t * n_k, n_k), n_k)

            @pl.when(j > 0)
            def _():
                remote(
                    spec_out.at[q, rows_out], spec_in.at[q, :, at, :], b_send.at[q], b_recv.at[q], (pt, h)
                ).start()

            @pl.when(j == 0)
            def _():
                pltpu.make_async_copy(spec_out.at[q, rows_out], spec_in.at[q, :, at, :], b_own.at[q]).start()

    pl.loop(0, n_half)(spread)

    def finish(q):
        lanes = pl.ds(pl.multiple_of(q * LANES, LANES), LANES)
        mine = pl.ds(0, n_k)
        rest = pl.ds(0, (n_tok - 1) * n_k)
        pltpu.make_async_copy(spec_in.at[q, :, mine, :], spec_in.at[q, :, mine, :], b_own.at[q]).wait()
        pltpu.make_async_copy(spec_in.at[q, :, rest, :], spec_in.at[q, :, rest, :], b_recv.at[q]).wait()

        @pl.loop(0, local // 2)
        def _(ip):
            two = jnp.concatenate([spec_in[q, 2 * ip + i] for i in range(2)], axis=1)
            got = dot(mats[2], two).astype(BF16)
            for i in range(2):
                at = pl.ds(pl.multiple_of((2 * ip + i) * block, block), block)
                result[at, lanes] = got[:, i * LANES : (i + 1) * LANES]

            @pl.when(q == n_half - 1)
            def _():
                both = pl.ds(pl.multiple_of(2 * ip * block, 2 * block), 2 * block)
                pltpu.make_async_copy(result.at[both], out.at[both], out_sem.at[ip]).start()

    pl.loop(0, n_half)(finish)

    @pl.loop(0, half)
    def _(r):
        cross(r).wait_send()
        partner(r).wait_send()
        forward(r).wait_send()

    for i in range(2):
        w_far(i).wait_send()
    sent = pl.ds(0, most)
    pltpu.make_async_copy(sec_in.at[sent], sec_in.at[sent], a_send).wait()
    for q in range(n_half):
        gone = pl.ds(0, (n_tok - 1) * local)
        pltpu.make_async_copy(spec_out.at[q, gone], spec_out.at[q, gone], b_send.at[q]).wait()

    @pl.loop(0, local // 2)
    def _(ip):
        both = pl.ds(pl.multiple_of(2 * ip * block, 2 * block), 2 * block)
        pltpu.make_async_copy(result.at[both], out.at[both], out_sem.at[ip]).wait()


def shards(
    tokens,
    w_value,
    w_gate,
    first_factor,
    twiddle,
    second_factor,
    freq_kernel,
    row_kernel,
    inverse_first,
    inverse_second,
):
    n_tok = lax.axis_size("tok")
    tok_rows, width = tokens.shape
    block = first_factor.shape[0]
    depth = w_value.shape[0]
    n_a = second_factor.shape[0]
    local = tok_rows // block
    half = local // 2
    n_k = block // n_tok
    n_half = width // LANES
    hbm, vmem = pl.BlockSpec(memory_space=pl.ANY), pl.BlockSpec(memory_space=pltpu.VMEM)
    dma = pltpu.SemaphoreType.DMA
    return pl.pallas_call(
        functools.partial(mixer, n_tok),
        out_shape=jax.ShapeDtypeStruct((tok_rows, width), BF16),
        in_specs=[hbm, hbm, hbm, vmem, vmem, hbm, hbm, hbm, vmem, vmem],
        out_specs=hbm,
        scratch_shapes=[
            pltpu.VMEM((half, depth // width, block, width), BF16),
            pltpu.VMEM((2, 2, depth, width), BF16),
            pltpu.VMEM((half, 2, block, width), BF16),
            pltpu.VMEM((n_a, n_k, width), BF16),
            pltpu.VMEM((n_a * n_k, LANES), F32),
            pltpu.VMEM((n_a * n_k, LANES), F32),
            pltpu.VMEM((n_half, n_a, n_k, LANES), BF16),
            pltpu.VMEM((n_half, local, block, LANES), BF16),
            pltpu.VMEM((tok_rows, width), BF16),
            pltpu.VMEM((3, n_a, n_a), F32),
            pltpu.VMEM((3, n_a, n_a), BF16),
            dma((half,)), dma((half,)), dma((half,)), dma((half,)), dma((half,)), dma((half,)), dma((half,)),
            dma((2,)), dma((2,)), dma((2,)), dma((3,)),
            dma, dma, dma, dma((n_half,)), dma((n_half,)), dma((n_half,)), dma((local // 2,)),
        ],
        compiler_params=pltpu.CompilerParams(
            collective_id=0, has_side_effects=True, vmem_limit_bytes=62 * 2**20
        ),
    )(
        tokens, w_value, w_gate, first_factor, twiddle.T, second_factor, inverse_first, inverse_second,
        freq_kernel.reshape(n_k, n_half, 1, LANES), row_kernel,
    )


def solution(mesh):
    return jax.shard_map(
        shards,
        mesh=mesh,
        in_specs=(
            P("tok", "ch"),
            P(None, "ch"),
            P(None, "ch"),
            P(),
            P("tok", None),
            P(),
            P("tok", "ch"),
            P(None, "ch"),
            P(),
            P(),
        ),
        out_specs=P("tok", "ch"),
        check_vma=False,
    )
```

time: 588 us -> 172 us (0.29); the launches traced: 576 us -> 170 us
  waiting for transfers between devices: 285 us -> 0 us
  Pallas kernels: 0 us -> 162 us
  blocking collectives: 118 us -> 0 us
  matrix products: 109 us -> 0 us
  local copies, waits for them, and re-layouts: 39.6 us -> 7.39 us
  between operations: 13.7 us -> 0.01 us
  starting transfers between devices: 10.2 us -> 0 us
    pallas_call x0 -> x1, Pallas kernels: none -> 162 us  [shards(): pl.pallas_call(functools.partial(mixer, n_tok), out_shape=jax.ShapeDtypeS...]
    all_gather x1 -> x0, waiting for transfers between devices: 153 us -> none  [shards(): piece = lax.all_gather(tokens, 'ch', axis=1, tiled=True)]
    all_to_all x1 -> x0, waiting for transfers between devices: 131 us -> none  [shards(): lax.all_to_all(section, 'tok', split_axis=1, concat_axis=0, tiled=True)]
    all_to_all x1 -> x0, blocking collectives: 118 us -> none  [shards(): lax.all_to_all(spectrum, 'tok', split_axis=0, concat_axis=1, tiled=True)]
    dot_general x6 -> x0, matrix products: 109 us -> none  [the longest x1 30.9 us: shards(): jnp.einsum('ja,akc->jkc', second_factor, lax.all_to_all(section, 'tok', s...]
    all_to_all x2 -> x0, local copies, waits for them, and re-layouts: 12.4 us -> none  [the longest x1 10.9 us: shards(): lax.all_to_all(section, 'tok', split_axis=1, concat_axis=0, tiled=True)]
    mul x1 -> x0, local copies, waits for them, and re-layouts: 10.3 us -> none  [shards(): section = section * twiddle[:, :, None]]
    dot_general x1 -> x0, local copies, waits for them, and re-layouts: 10.3 us -> none  [shards(): jnp.einsum('ij,jkc->ikc', inverse_first, spectrum, precision=highest)]
  transfers between devices with their start and end apart: 2 -> 0, of which waited for: 2 -> 0; matrix products, arithmetic and copies ran while one was open for 0% -> 0% of each run, Pallas kernels for 0% -> 0%
where the time goes in v2:
time: 172 us; the launch traced here: 170 us
  Pallas kernels  162 us (94%)
  local copies, waits for them, and re-layouts  7.39 us (4%)
    pallas_call x1, Pallas kernels, shards(): pl.pallas_call(functools.partial(mixer, n_tok), out_shape=jax.ShapeDtypeS...  162 us
    unnamed x2, local copies, waits for them, and re-layouts  6.06 us

profile of v2, /device:TPU:0, one launch (start us, length us, event | category | flops | bytes accessed | tf_op | source)
XLA Modules:
  0.0 169.6 jit_solution(3969124038140527132)
XLA Ops:
  0.0 1.3 reshape.3.freq
  1.3 1.6 copy.11
  2.9 162.2 %shard_map.100 = bf16[8192,256]{1,0:T(8,128)(2,1)} custom-call(bf16[8192,256]{1,0:T(8,128)(2,1)} %tokens.1, bf16[1024,256]{1,0:T(8,128)(2,1)} %w_value.1, bf16[1024,256]{1,0:T(8,128)(2,1)} %w_gate.1, bf16[512,512]{1,0:T(8,128)(2,1)} %first.1, f32[512,16]{1,0:T(8,128)} %bitcast.1, f32[512,512]{1,0:T(8,128)} %second.1, f32[512,512]{1,0:T(8,128)} %inv_one.1, ...), custom_call_target="tpu_custom_call" | custom-call | tf_op jit(solution)/shard_map/pallas_call | solution.py:260
  165.2 4.5 %copy.13 = bf16[8192,256]{1,0:T(8,128)(2,1)} copy(bf16[8192,256]{1,0:T(8,128)(2,1)} %shard_map.100) | data formatting | bytes 8388608

commit v3 on v2

v3 whole, which is shorter than its diff:
```python
import functools

import jax
import jax.numpy as jnp
from jax import lax
from jax.experimental import pallas as pl
from jax.experimental.pallas import tpu as pltpu
from jax.sharding import PartitionSpec as P

MESH = pl.DeviceIdType.MESH
LANES = 128
F32, BF16 = jnp.float32, jnp.bfloat16


def dot(a, b):
    return jnp.dot(a, b, preferred_element_type=F32)


def flip(index, bit):
    return index + bit - 2 * bit * ((index // bit) % 2)


def mixer(
    n_tok,
    tokens, w_value, w_gate, first, twiddle, second, inv_one, inv_two, freq, row_kernel,
    out,
    x, w, sec_out, sec_in, wide_in, wide_out, spec_out, spec_in, result,
    wide_mats, mats, first_mat, twiddle_raw, twiddle_cols, freq_raw, freq_rows, row_mat,
    cross_s, cross_r, core_s, core_r, fwd_s, fwd_r, own_sem, w_sem, ws_sem, wr_sem, small_sem,
    known, a_send, a_recv, a_own, b_send, b_recv, b_own, out_sem,
):
    t, h = lax.axis_index("tok"), lax.axis_index("ch")
    lo, core = h // 2, h % 2
    half, pieces, block, width = x.shape
    n_half, n_a, n_k, _ = sec_in.shape
    local = 2 * half
    me = t * 2 + lo
    y_dev = (t, flip(h, 2))
    core_dev = (t, flip(h, 1))
    w_dev = (flip(t, 1), flip(h, 2))
    far, far_core, near = flip(h, 2), flip(flip(h, 2), 1), flip(h, 1)
    bits = [2**i for i in range(n_tok.bit_length() - 1)]
    links = [y_dev] + [(flip(t, b), h) for b in bits]

    barrier = pltpu.get_barrier_semaphore()
    close = links + [core_dev, w_dev]
    for d in close:
        pl.semaphore_signal(barrier, inc=1, device_id=d, device_id_type=MESH)

    def remote(src, dst, s, r, dev):
        return pltpu.make_async_remote_copy(
            src_ref=src, dst_ref=dst, send_sem=s, recv_sem=r, device_id=dev, device_id_type=MESH
        )

    def rows(at, r):
        return tokens.at[pl.ds(pl.multiple_of((at * half + r) * block, block), block), :]

    def cross(r):
        return remote(rows(1 - lo, r), x.at[r, h], cross_s.at[r], cross_r.at[r], y_dev)

    def partner(r):
        return remote(rows(lo, r), x.at[r, h], core_s.at[r], core_r.at[r], core_dev)

    def own(r):
        return pltpu.make_async_copy(rows(lo, r), x.at[r, h], own_sem.at[r])

    def forward(r):
        return remote(x.at[r, far], x.at[r, far], fwd_s.at[r], fwd_r.at[r], core_dev)

    def w_own(i):
        return pltpu.make_async_copy((w_value, w_gate)[i], w.at[lo, i], w_sem.at[i])

    def w_far(i):
        return remote((w_value, w_gate)[i], w.at[lo, i], ws_sem.at[i], wr_sem.at[i], w_dev)

    def arrived(r, piece, sem):
        pltpu.make_async_copy(x.at[r, piece], x.at[r, piece], sem.at[r]).wait()

    small = [
        (twiddle, twiddle_raw), (first, first_mat), (freq, freq_raw), (second, wide_mats.at[0]),
        (inv_one, wide_mats.at[1]), (inv_two, wide_mats.at[2]), (row_kernel, row_mat),
    ]
    loads = [pltpu.make_async_copy(a, b, small_sem.at[i]) for i, (a, b) in enumerate(small)]
    for i in range(2):
        w_own(i).start()
    for load in loads:
        load.start()

    pl.semaphore_wait(barrier, len(close))

    @pl.loop(0, half)
    def _(r):
        cross(r).start()

    for i in range(2):
        w_far(i).start()

    @pl.loop(0, half)
    def _(r):
        own(r).start()
        partner(r).start()

    for i, d in enumerate(links):
        pl.semaphore_signal(known.at[i], inc=1, device_id=d, device_id_type=MESH)
        pl.semaphore_wait(known.at[i], 1)

    for load in loads:
        load.wait()
    same = lax.broadcasted_iota(jnp.int32, (block, block), 0) == lax.broadcasted_iota(
        jnp.int32, (block, block), 1
    )

    @pl.loop(0, half)
    def _(r):
        row = twiddle_raw[pl.ds(pl.multiple_of(lo * half, half), half), :]
        pick = lax.broadcasted_iota(jnp.int32, row.shape, 0) == r
        row = jnp.sum(jnp.where(pick, row, 0.0), axis=0, keepdims=True)
        column = jnp.sum(jnp.where(same, row, 0.0), axis=1, keepdims=True)
        twiddle_cols[r] = jnp.broadcast_to(column, (block, LANES))

    for k in range(n_k):
        for q in range(n_half):
            freq_rows[k, q] = freq_raw[k : k + 1, q * LANES : (q + 1) * LANES]
    for i in range(3):
        high = wide_mats[i].astype(BF16)
        mats[i, 0] = high
        mats[i, 1] = (wide_mats[i] - high.astype(F32)).astype(BF16)
    for i in range(2):
        w_own(i).wait()

    def block_of(p):
        return pl.ds(pl.multiple_of(p * n_k, n_k), n_k)

    def send_section(q, r, n):
        at, to = pl.ds(r, n), pl.ds(t * local + lo * half + r, n)

        @pl.loop(1, 2 * n_tok)
        def _(j):
            p = (me + j * 27) % (2 * n_tok)
            remote(
                sec_out.at[q, at, p % 2, block_of(p // 2), :], sec_in.at[q, to],
                a_send.at[q], a_recv.at[q], (p // 2, (p % 2) * 2 + core),
            ).start()

        pltpu.make_async_copy(
            sec_out.at[q, at, lo, block_of(t), :], sec_in.at[q, to], a_own.at[q]
        ).start()

    def project(step):
        q = half // 2
        early = step < q
        middle = (step >= q) & (step < 2 * q)
        late = step - 2 * q
        r = jnp.where(early, step, jnp.where(middle, step - q, q + late // 2))
        other = jnp.where(early, 0, jnp.where(middle, 1, late % 2))
        l = lo + other - 2 * lo * other

        @pl.when(step == q)
        def _():
            for i in range(2):
                pltpu.make_async_copy(w.at[1 - lo, i], w.at[1 - lo, i], wr_sem.at[i]).wait()

        @pl.when(other == 0)
        def _():
            arrived(r, far, cross_r)
            forward(r).start()
            own(r).wait()
            arrived(r, near, core_r)
            arrived(r, far_core, fwd_r)

        row = jnp.concatenate([x[r, p] for p in range(pieces)], axis=1)
        value = dot(row, w[l, 0])
        gate = dot(row, w[l, 1])
        gated = (value * (gate / (1.0 + jnp.exp(-gate)))).astype(BF16)
        section = dot(first_mat[...], gated)
        for i in range(n_half):
            sec_out[i, r, l] = (section[:, i * LANES : (i + 1) * LANES] * twiddle_cols[r]).astype(BF16)

        @pl.when((other == 1) & (r % 2 == 1))
        def _():
            send_section(0, r - 1, 2)

    pl.loop(0, 2 * half)(project)
    for q in range(1, n_half):
        send_section(q, 0, half)

    most = pl.ds(0, n_a - half)
    step_a = 32
    quarter = local // 2

    def spread(q):
        lanes = pl.ds(pl.multiple_of(q * LANES, LANES), LANES)
        mine = sec_in.at[q, pl.ds(0, half)]
        pltpu.make_async_copy(mine, mine, a_own.at[q]).wait()
        pltpu.make_async_copy(sec_in.at[q, most], sec_in.at[q, most], a_recv.at[q]).wait()

        @pl.loop(0, n_a // step_a)
        def _(i):
            part = sec_in[q, pl.ds(i * step_a, step_a)].astype(F32)
            wide_in[pl.ds(pl.multiple_of(i * step_a * n_k, step_a * n_k), step_a * n_k), :] = part.reshape(
                step_a * n_k, LANES
            )

        @pl.loop(0, n_k // 2)
        def _(kp):
            two = [wide_in[pl.ds(2 * kp + i, n_a, stride=n_k), :].astype(BF16) for i in range(2)]
            two = jnp.concatenate(two, axis=1)
            mid = dot(mats[0, 0], two) + dot(mats[0, 1], two)
            scale = [freq_rows[2 * kp + i, q] * row_mat[:, lanes] for i in range(2)]
            mid = (mid * jnp.concatenate(scale, axis=1)).astype(BF16)
            end = dot(mats[1, 0], mid) + dot(mats[1, 1], mid)
            for i in range(2):
                wide_out[pl.ds(2 * kp + i, n_a, stride=n_k), :] = end[:, i * LANES : (i + 1) * LANES]

        for part in range(2):

            @pl.loop(0, n_tok)
            def _(j):
                pt = (t + j * 13) % n_tok
                first_row = pl.multiple_of(pt * local + part * quarter, quarter)
                rows_out = pl.ds(first_row, quarter)
                flat = pl.ds(pl.multiple_of(first_row * n_k, quarter * n_k), quarter * n_k)
                spec_out[q, rows_out] = wide_out[flat, :].astype(BF16).reshape(quarter, n_k, LANES)
                to = spec_in.at[q, pl.ds(part * quarter, quarter), block_of(t), :]

                @pl.when(j > 0)
                def _():
                    remote(
                        spec_out.at[q, rows_out], to, b_send.at[q, part], b_recv.at[q, part], (pt, h)
                    ).start()

                @pl.when(j == 0)
                def _():
                    pltpu.make_async_copy(spec_out.at[q, rows_out], to, b_own.at[q, part]).start()

    pl.loop(0, n_half)(spread)

    def both(ip):
        return pl.ds(pl.multiple_of(2 * ip * block, 2 * block), 2 * block)

    def finish(step):
        q, part = step // 2, step % 2
        lanes = pl.ds(pl.multiple_of(q * LANES, LANES), LANES)
        at = pl.ds(pl.multiple_of(part * quarter, quarter), quarter)
        mine = spec_in.at[q, at, pl.ds(0, n_k), :]
        rest = spec_in.at[q, at, pl.ds(0, (n_tok - 1) * n_k), :]
        pltpu.make_async_copy(mine, mine, b_own.at[q, part]).wait()
        pltpu.make_async_copy(rest, rest, b_recv.at[q, part]).wait()

        @pl.loop(0, quarter // 2)
        def _(i):
            ip = part * (quarter // 2) + i
            two = jnp.concatenate([spec_in[q, 2 * ip + i] for i in range(2)], axis=1)
            got = dot(mats[2, 0], two).astype(BF16)
            for i in range(2):
                here = pl.ds(pl.multiple_of((2 * ip + i) * block, block), block)
                result[here, lanes] = got[:, i * LANES : (i + 1) * LANES]

            @pl.when(q == n_half - 1)
            def _():
                pltpu.make_async_copy(result.at[both(ip)], out.at[both(ip)], out_sem.at[ip]).start()

    pl.loop(0, 2 * n_half)(finish)

    @pl.loop(0, half)
    def _(r):
        cross(r).wait_send()
        partner(r).wait_send()
        forward(r).wait_send()

    for i in range(2):
        w_far(i).wait_send()
    for q in range(n_half):
        pltpu.make_async_copy(sec_in.at[q, most], sec_in.at[q, most], a_send.at[q]).wait()
        for part in range(2):
            gone = spec_out.at[q, pl.ds(0, (n_tok - 1) * quarter)]
            pltpu.make_async_copy(gone, gone, b_send.at[q, part]).wait()

    @pl.loop(0, local // 2)
    def _(ip):
        pltpu.make_async_copy(result.at[both(ip)], out.at[both(ip)], out_sem.at[ip]).wait()


def shards(
    tokens,
    w_value,
    w_gate,
    first_factor,
    twiddle,
    second_factor,
    freq_kernel,
    row_kernel,
    inverse_first,
    inverse_second,
):
    n_tok = lax.axis_size("tok")
    tok_rows, width = tokens.shape
    block = first_factor.shape[0]
    depth = w_value.shape[0]
    n_a = second_factor.shape[0]
    local = tok_rows // block
    half = local // 2
    n_k = block // n_tok
    n_half = width // LANES
    hbm = pl.BlockSpec(memory_space=pl.ANY)
    dma = pltpu.SemaphoreType.DMA
    return pl.pallas_call(
        functools.partial(mixer, n_tok),
        out_shape=jax.ShapeDtypeStruct((tok_rows, width), BF16),
        in_specs=[hbm] * 10,
        out_specs=hbm,
        scratch_shapes=[
            pltpu.VMEM((half, depth // width, block, width), BF16),
            pltpu.VMEM((2, 2, depth, width), BF16),
            pltpu.VMEM((n_half, half, 2, block, LANES), BF16),
            pltpu.VMEM((n_half, n_a, n_k, LANES), BF16),
            pltpu.VMEM((n_a * n_k, LANES), F32),
            pltpu.VMEM((n_a * n_k, LANES), F32),
            pltpu.VMEM((n_half, n_a, n_k, LANES), BF16),
            pltpu.VMEM((n_half, local, block, LANES), BF16),
            pltpu.VMEM((tok_rows, width), BF16),
            pltpu.VMEM((3, n_a, n_a), F32),
            pltpu.VMEM((3, 2, n_a, n_a), BF16),
            pltpu.VMEM((block, block), BF16),
            pltpu.VMEM((local, block), F32),
            pltpu.VMEM((half, block, LANES), F32),
            pltpu.VMEM((n_k, width), F32),
            pltpu.VMEM((n_k, n_half, 1, LANES), F32),
            pltpu.VMEM((n_a, width), F32),
            dma((half,)), dma((half,)), dma((half,)), dma((half,)), dma((half,)), dma((half,)), dma((half,)),
            dma((2,)), dma((2,)), dma((2,)), dma((7,)),
            pltpu.SemaphoreType.REGULAR((n_tok.bit_length(),)),
            dma((n_half,)), dma((n_half,)), dma((n_half,)),
            dma((n_half, 2)), dma((n_half, 2)), dma((n_half, 2)), dma((local // 2,)),
        ],
        compiler_params=pltpu.CompilerParams(
            collective_id=0, has_side_effects=True, vmem_limit_bytes=63 * 2**20
        ),
    )(
        tokens, w_value, w_gate, first_factor, twiddle, second_factor, inverse_first, inverse_second,
        freq_kernel, row_kernel,
    )


def solution(mesh):
    return jax.shard_map(
        shards,
        mesh=mesh,
        in_specs=(
            P("tok", "ch"),
            P(None, "ch"),
            P(None, "ch"),
            P(),
            P("tok", None),
            P(),
            P("tok", "ch"),
            P(None, "ch"),
            P(),
            P(),
        ),
        out_specs=P("tok", "ch"),
        check_vma=False,
    )
```

time: 172 us -> 156 us (0.907)
  Pallas kernels: 162 us -> 150 us
  local copies, waits for them, and re-layouts: 7.39 us -> 4.47 us
    pallas_call x1, Pallas kernels: 162 us -> 150 us  [shards(): pl.pallas_call(functools.partial(mixer, n_tok), out_shape=jax.ShapeDtypeS...]
    unnamed x2 -> x1, local copies, waits for them, and re-layouts: 6.06 us -> 4.47 us
where the time goes in v3:
time: 156 us; the launch traced here: 154 us
  Pallas kernels  150 us (96%)
  local copies, waits for them, and re-layouts  4.47 us (3%)
    pallas_call x1, Pallas kernels, shards(): pl.pallas_call(functools.partial(mixer, n_tok), out_shape=jax.ShapeDtypeS...  150 us
    unnamed x1, local copies, waits for them, and re-layouts  4.47 us

profile of v3, /device:TPU:0, one launch (start us, length us, event | category | flops | bytes accessed | tf_op | source)
XLA Modules:
  0.0 154.4 jit_solution(5907623135320798463)
XLA Ops:
  0.0 149.9 %shard_map.100 = bf16[8192,256]{1,0:T(8,128)(2,1)} custom-call(bf16[8192,256]{1,0:T(8,128)(2,1)} %tokens.1, bf16[1024,256]{1,0:T(8,128)(2,1)} %w_value.1, bf16[1024,256]{1,0:T(8,128)(2,1)} %w_gate.1, bf16[512,512]{1,0:T(8,128)(2,1)} %first.1, f32[16,512]{1,0:T(8,128)} %twiddle.1, f32[512,512]{1,0:T(8,128)} %second.1, f32[512,512]{1,0:T(8,128)} %inv_one.1, ...), custom_call_target="tpu_custom_call" | custom-call | tf_op jit(solution)/shard_map/pallas_call | solution.py:307
  149.9 4.5 %copy.12 = bf16[8192,256]{1,0:T(8,128)(2,1)} copy(bf16[8192,256]{1,0:T(8,128)(2,1)} %shard_map.100) | data formatting | bytes 8388608

commit v4 on v3

--- a/solution.py
+++ b/solution.py
@@ -216,7 +216,7 @@
 
             @pl.loop(0, n_tok)
             def _(j):
-                pt = (t + j * 13) % n_tok
+                pt = (t + j * 5) % n_tok
                 first_row = pl.multiple_of(pt * local + part * quarter, quarter)
                 rows_out = pl.ds(first_row, quarter)
                 flat = pl.ds(pl.multiple_of(first_row * n_k, quarter * n_k), quarter * n_k)
@@ -306,7 +306,7 @@
     dma = pltpu.SemaphoreType.DMA
     return pl.pallas_call(
         functools.partial(mixer, n_tok),
-        out_shape=jax.ShapeDtypeStruct((tok_rows, width), BF16),
+        out_shape=pltpu.VMEM((tok_rows, width), BF16),
         in_specs=[hbm] * 10,
         out_specs=hbm,
         scratch_shapes=[
@@ -334,7 +334,7 @@
             dma((n_half, 2)), dma((n_half, 2)), dma((n_half, 2)), dma((local // 2,)),
         ],
         compiler_params=pltpu.CompilerParams(
-            collective_id=0, has_side_effects=True, vmem_limit_bytes=63 * 2**20
+            collective_id=0, has_side_effects=True, vmem_limit_bytes=56 * 2**20
         ),
     )(
         tokens, w_value, w_gate, first_factor, twiddle, second_factor, inverse_first, inverse_second,

time: 156 us -> 153 us (0.981)
  local copies, waits for them, and re-layouts: 4.47 us -> 2.02 us
    unnamed x1, local copies, waits for them, and re-layouts: 4.47 us -> 2.02 us
where the time goes in v4:
time: 153 us; the launch traced here: 151 us
  Pallas kernels  149 us (97%)
  local copies, waits for them, and re-layouts  2.02 us (1%)
    pallas_call x1, Pallas kernels, shards(): pl.pallas_call(functools.partial(mixer, n_tok), out_shape=pltpu.VMEM((tok...  149 us

profile of v4, /device:TPU:0, one launch (start us, length us, event | category | flops | bytes accessed | tf_op | source)
XLA Modules:
  0.0 150.9 jit_solution(315796967992218688)
XLA Ops:
  0.0 148.9 %shard_map.100 = bf16[8192,256]{1,0:T(8,128)(2,1)S(1)} custom-call(bf16[8192,256]{1,0:T(8,128)(2,1)} %tokens.1, bf16[1024,256]{1,0:T(8,128)(2,1)} %w_value.1, bf16[1024,256]{1,0:T(8,128)(2,1)} %w_gate.1, bf16[512,512]{1,0:T(8,128)(2,1)} %first.1, f32[16,512]{1,0:T(8,128)} %twiddle.1, f32[512,512]{1,0:T(8,128)} %second.1, f32[512,512]{1,0:T(8,128)} %inv_one.1, ...), custom_call_target="tpu_custom_call" | custom-call | tf_op jit(solution)/shard_map/pallas_call | solution.py:307
  148.9 2.0 %copy.12 = bf16[8192,256]{1,0:T(8,128)(2,1)} copy(bf16[8192,256]{1,0:T(8,128)(2,1)S(1)} %shard_map.100) | data formatting | bytes 8388608

commit v5 on v4

--- a/solution.py
+++ b/solution.py
@@ -23,11 +23,11 @@
 def mixer(
     n_tok,
     tokens, w_value, w_gate, first, twiddle, second, inv_one, inv_two, freq, row_kernel,
-    out,
-    x, w, sec_out, sec_in, wide_in, wide_out, spec_out, spec_in, result,
+    result,
+    x, w, sec_out, sec_in, wide_in, wide_out, spec_out, spec_in,
     wide_mats, mats, first_mat, twiddle_raw, twiddle_cols, freq_raw, freq_rows, row_mat,
     cross_s, cross_r, core_s, core_r, fwd_s, fwd_r, own_sem, w_sem, ws_sem, wr_sem, small_sem,
-    known, a_send, a_recv, a_own, b_send, b_recv, b_own, out_sem,
+    known, a_send, a_recv, a_own, b_send, b_recv, b_own,
 ):
     t, h = lax.axis_index("tok"), lax.axis_index("ch")
     lo, core = h // 2, h % 2
@@ -186,7 +186,8 @@
 
     most = pl.ds(0, n_a - half)
     step_a = 32
-    quarter = local // 2
+    n_part = b_send.shape[1]
+    quarter = local // n_part
 
     def spread(q):
         lanes = pl.ds(pl.multiple_of(q * LANES, LANES), LANES)
@@ -212,7 +213,7 @@
             for i in range(2):
                 wide_out[pl.ds(2 * kp + i, n_a, stride=n_k), :] = end[:, i * LANES : (i + 1) * LANES]
 
-        for part in range(2):
+        for part in range(n_part):
 
             @pl.loop(0, n_tok)
             def _(j):
@@ -235,11 +236,8 @@
 
     pl.loop(0, n_half)(spread)
 
-    def both(ip):
-        return pl.ds(pl.multiple_of(2 * ip * block, 2 * block), 2 * block)
-
     def finish(step):
-        q, part = step // 2, step % 2
+        q, part = step // n_part, step % n_part
         lanes = pl.ds(pl.multiple_of(q * LANES, LANES), LANES)
         at = pl.ds(pl.multiple_of(part * quarter, quarter), quarter)
         mine = spec_in.at[q, at, pl.ds(0, n_k), :]
@@ -256,11 +254,7 @@
                 here = pl.ds(pl.multiple_of((2 * ip + i) * block, block), block)
                 result[here, lanes] = got[:, i * LANES : (i + 1) * LANES]
 
-            @pl.when(q == n_half - 1)
-            def _():
-                pltpu.make_async_copy(result.at[both(ip)], out.at[both(ip)], out_sem.at[ip]).start()
-
-    pl.loop(0, 2 * n_half)(finish)
+    pl.loop(0, n_part * n_half)(finish)
 
     @pl.loop(0, half)
     def _(r):
@@ -272,13 +266,9 @@
         w_far(i).wait_send()
     for q in range(n_half):
         pltpu.make_async_copy(sec_in.at[q, most], sec_in.at[q, most], a_send.at[q]).wait()
-        for part in range(2):
+        for part in range(n_part):
             gone = spec_out.at[q, pl.ds(0, (n_tok - 1) * quarter)]
             pltpu.make_async_copy(gone, gone, b_send.at[q, part]).wait()
-
-    @pl.loop(0, local // 2)
-    def _(ip):
-        pltpu.make_async_copy(result.at[both(ip)], out.at[both(ip)], out_sem.at[ip]).wait()
 
 
 def shards(
@@ -308,7 +298,7 @@
         functools.partial(mixer, n_tok),
         out_shape=pltpu.VMEM((tok_rows, width), BF16),
         in_specs=[hbm] * 10,
-        out_specs=hbm,
+        out_specs=pl.BlockSpec(memory_space=pltpu.VMEM),
         scratch_shapes=[
             pltpu.VMEM((half, depth // width, block, width), BF16),
             pltpu.VMEM((2, 2, depth, width), BF16),
@@ -318,7 +308,6 @@
             pltpu.VMEM((n_a * n_k, LANES), F32),
             pltpu.VMEM((n_half, n_a, n_k, LANES), BF16),
             pltpu.VMEM((n_half, local, block, LANES), BF16),
-            pltpu.VMEM((tok_rows, width), BF16),
             pltpu.VMEM((3, n_a, n_a), F32),
             pltpu.VMEM((3, 2, n_a, n_a), BF16),
             pltpu.VMEM((block, block), BF16),
@@ -331,10 +320,10 @@
             dma((2,)), dma((2,)), dma((2,)), dma((7,)),
             pltpu.SemaphoreType.REGULAR((n_tok.bit_length(),)),
             dma((n_half,)), dma((n_half,)), dma((n_half,)),
-            dma((n_half, 2)), dma((n_half, 2)), dma((n_half, 2)), dma((local // 2,)),
+            dma((n_half, 4)), dma((n_half, 4)), dma((n_half, 4)),
         ],
         compiler_params=pltpu.CompilerParams(
-            collective_id=0, has_side_effects=True, vmem_limit_bytes=56 * 2**20
+            collective_id=0, has_side_effects=True, vmem_limit_bytes=52 * 2**20
         ),
     )(
         tokens, w_value, w_gate, first_factor, twiddle, second_factor, inverse_first, inverse_second,

time: 153 us -> 152 us (level)
  no operation moved by 1% of the time
where the time goes in v5:
time: 152 us; the launch traced here: 150 us
  Pallas kernels  148 us (97%)
  local copies, waits for them, and re-layouts  2.02 us (1%)
    pallas_call x1, Pallas kernels, shards(): pl.pallas_call(functools.partial(mixer, n_tok), out_shape=pltpu.VMEM((tok...  148 us

profile of v5, /device:TPU:0, one launch (start us, length us, event | category | flops | bytes accessed | tf_op | source)
XLA Modules:
  0.0 150.1 jit_solution(14183258177844584078)
XLA Ops:
  0.0 148.1 %shard_map.100 = bf16[8192,256]{1,0:T(8,128)(2,1)S(1)} custom-call(bf16[8192,256]{1,0:T(8,128)(2,1)} %tokens.1, bf16[1024,256]{1,0:T(8,128)(2,1)} %w_value.1, bf16[1024,256]{1,0:T(8,128)(2,1)} %w_gate.1, bf16[512,512]{1,0:T(8,128)(2,1)} %first.1, f32[16,512]{1,0:T(8,128)} %twiddle.1, f32[512,512]{1,0:T(8,128)} %second.1, f32[512,512]{1,0:T(8,128)} %inv_one.1, ...), custom_call_target="tpu_custom_call" | custom-call | tf_op jit(solution)/shard_map/pallas_call | solution.py:297
  148.1 2.0 %copy.12 = bf16[8192,256]{1,0:T(8,128)(2,1)} copy(bf16[8192,256]{1,0:T(8,128)(2,1)S(1)} %shard_map.100) | data formatting | bytes 8388608

commit v6 on v5

--- a/solution.py
+++ b/solution.py
@@ -100,10 +100,6 @@
         own(r).start()
         partner(r).start()
 
-    for i, d in enumerate(links):
-        pl.semaphore_signal(known.at[i], inc=1, device_id=d, device_id_type=MESH)
-        pl.semaphore_wait(known.at[i], 1)
-
     for load in loads:
         load.wait()
     same = lax.broadcasted_iota(jnp.int32, (block, block), 0) == lax.broadcasted_iota(
@@ -128,6 +124,10 @@
     for i in range(2):
         w_own(i).wait()
 
+    for i, d in enumerate(links):
+        pl.semaphore_signal(known.at[i], inc=1, device_id=d, device_id_type=MESH)
+        pl.semaphore_wait(known.at[i], 1)
+
     def block_of(p):
         return pl.ds(pl.multiple_of(p * n_k, n_k), n_k)
 
@@ -136,7 +136,7 @@
 
         @pl.loop(1, 2 * n_tok)
         def _(j):
-            p = (me + j * 27) % (2 * n_tok)
+            p = (me + j * 39) % (2 * n_tok)
             remote(
                 sec_out.at[q, at, p % 2, block_of(p // 2), :], sec_in.at[q, to],
                 a_send.at[q], a_recv.at[q], (p // 2, (p % 2) * 2 + core),
@@ -147,7 +147,7 @@
         ).start()
 
     def project(step):
-        q = half // 2
+        q = half * 3 // 8
         early = step < q
         middle = (step >= q) & (step < 2 * q)
         late = step - 2 * q
@@ -185,7 +185,7 @@
         send_section(q, 0, half)
 
     most = pl.ds(0, n_a - half)
-    step_a = 32
+    step_a = 64
     n_part = b_send.shape[1]
     quarter = local // n_part
 

time: 152 us -> 152 us (level)
  no operation moved by 1% of the time
where the time goes in v6:
time: 152 us; the launch traced here: 150 us
  Pallas kernels  148 us (97%)
  local copies, waits for them, and re-layouts  2.02 us (1%)
    pallas_call x1, Pallas kernels, shards(): pl.pallas_call(functools.partial(mixer, n_tok), out_shape=pltpu.VMEM((tok...  148 us

profile of v6, /device:TPU:0, one launch (start us, length us, event | category | flops | bytes accessed | tf_op | source)
XLA Modules:
  0.0 150.1 jit_solution(13867458345187616102)
XLA Ops:
  0.0 148.1 %shard_map.100 = bf16[8192,256]{1,0:T(8,128)(2,1)S(1)} custom-call(bf16[8192,256]{1,0:T(8,128)(2,1)} %tokens.1, bf16[1024,256]{1,0:T(8,128)(2,1)} %w_value.1, bf16[1024,256]{1,0:T(8,128)(2,1)} %w_gate.1, bf16[512,512]{1,0:T(8,128)(2,1)} %first.1, f32[16,512]{1,0:T(8,128)} %twiddle.1, f32[512,512]{1,0:T(8,128)} %second.1, f32[512,512]{1,0:T(8,128)} %inv_one.1, ...), custom_call_target="tpu_custom_call" | custom-call | tf_op jit(solution)/shard_map/pallas_call | solution.py:297
  148.1 2.0 %copy.12 = bf16[8192,256]{1,0:T(8,128)(2,1)} copy(bf16[8192,256]{1,0:T(8,128)(2,1)S(1)} %shard_map.100) | data formatting | bytes 8388608

commit v7 on v6

--- a/solution.py
+++ b/solution.py
@@ -88,12 +88,12 @@
 
     pl.semaphore_wait(barrier, len(close))
 
+    for i in range(2):
+        w_far(i).start()
+
     @pl.loop(0, half)
     def _(r):
         cross(r).start()
-
-    for i in range(2):
-        w_far(i).start()
 
     @pl.loop(0, half)
     def _(r):

time: 152 us -> 152 us (level)
  no operation moved by 1% of the time
where the time goes in v7:
time: 152 us; the launch traced here: 150 us
  Pallas kernels  148 us (97%)
  local copies, waits for them, and re-layouts  2.02 us (1%)
    pallas_call x1, Pallas kernels, shards(): pl.pallas_call(functools.partial(mixer, n_tok), out_shape=pltpu.VMEM((tok...  148 us

profile of v7, /device:TPU:0, one launch (start us, length us, event | category | flops | bytes accessed | tf_op | source)
XLA Modules:
  0.0 150.0 jit_solution(6561032246419512894)
XLA Ops:
  0.0 148.0 %shard_map.100 = bf16[8192,256]{1,0:T(8,128)(2,1)S(1)} custom-call(bf16[8192,256]{1,0:T(8,128)(2,1)} %tokens.1, bf16[1024,256]{1,0:T(8,128)(2,1)} %w_value.1, bf16[1024,256]{1,0:T(8,128)(2,1)} %w_gate.1, bf16[512,512]{1,0:T(8,128)(2,1)} %first.1, f32[16,512]{1,0:T(8,128)} %twiddle.1, f32[512,512]{1,0:T(8,128)} %second.1, f32[512,512]{1,0:T(8,128)} %inv_one.1, ...), custom_call_target="tpu_custom_call" | custom-call | tf_op jit(solution)/shard_map/pallas_call | solution.py:297
  148.0 2.0 %copy.12 = bf16[8192,256]{1,0:T(8,128)(2,1)} copy(bf16[8192,256]{1,0:T(8,128)(2,1)S(1)} %shard_map.100) | data formatting | bytes 8388608
